TPU v7x, 32 devices: a whole 2x2x4 slice. The times are simulated.
32 devices in a mesh: occ: 4 (over y, x), vir: 8 (over z, core).
Axes of the slice: x: 2, y: 2, z: 4, core: 2. Of those that a mesh axis runs over, the one named last changes fastest.
Arguments:
- amplitudes: bfloat16 [1504, 3072], P('occ', 'vir'), may hold values from -6 to 6
- integrals: bfloat16 [3072, 3072], P(None, 'vir'), may hold values from -0.15625 to 0.15625
- tile_block: int32 [24], replicated, may hold values from 0 to 5, as said below
- pair_mask: int32 [6, 6], replicated, may hold values 0 or 1
- partner: int32 [1504], P('occ'), may hold values from 0 to 1503, as said below
Outputs:
- residual: float32 [1504, 3072], P('occ', 'vir')
Inputs may be any that keep to these rules, and one draw needn't show every extreme that they name: partner is an involution without fixed points: partner[partner[r]] = r and partner[r] != r. tile_block never falls along the tiles, and each of the 6 blocks holds at least one tile.
All inputs are finite; a program needn't handle non-finite values.
Results may differ from a plain program's by a relative error of at most 0.0003.
Values may be sent and summed in bfloat16 or wider, within the bound.
No kernel may reach another device: no remote copies, remote signals or barrier semaphores. Data moves between devices by JAX's collectives and lax.ppermute only.
A program may use at most 128 MiB of HBM per device.

v0:
```python
import jax
import jax.numpy as jnp
from jax import lax
from jax.sharding import PartitionSpec as P

TILE = 128


def body(amplitudes, integrals, tile_block, pair_mask, partner):
    columns = integrals.shape[1]
    local_tiles = columns // TILE
    total_tiles = tile_block.shape[0]
    groups = pair_mask.shape[0]
    first_tile = lax.axis_index("vir") * local_tiles
    own_blocks = lax.dynamic_slice_in_dim(tile_block, first_tile, local_tiles)
    labels = jnp.arange(groups, dtype=jnp.int32)
    row_onehot = (tile_block[:, None] == labels[None, :]).astype(jnp.float32)
    col_onehot = (own_blocks[:, None] == labels[None, :]).astype(jnp.float32)
    live_tiles = jnp.dot(jnp.dot(row_onehot, pair_mask.astype(jnp.float32)), col_onehot.T)
    masked = (
        integrals.reshape(total_tiles, TILE, local_tiles, TILE)
        * live_tiles.astype(jnp.bfloat16)[:, None, :, None]
    )
    masked = masked.reshape(integrals.shape)
    own_count = amplitudes.shape[0]
    gathered = lax.all_gather(amplitudes, "occ", axis=0, tiled=True)
    partner_rows = jnp.take(gathered, partner, axis=0)
    stacked = jnp.concatenate((amplitudes, partner_rows), axis=0)
    pair_sums = jnp.dot(
        lax.all_gather(stacked, "vir", axis=1, tiled=True),
        masked,
        preferred_element_type=jnp.float32,
    )
    residual = pair_sums[:own_count] - pair_sums[own_count:]
    return residual


def solution(mesh):
    placed = (P("occ", "vir"), P(None, "vir"), P(), P(), P("occ"))
    return jax.shard_map(
        body, mesh=mesh, in_specs=placed, out_specs=P("occ", "vir"), check_vma=False
    )
```

profile of v0, /device:TPU:0, one launch (start us, length us, event | category | flops | bytes accessed | tf_op | source)
XLA Modules:
  0.0 107.5 jit_solution(9422348159117418414)
XLA Ops:
  6.5 0.0 copy-start.2
  6.5 0.0 all-gather.3.cloned.1.call-start
  6.5 0.7 all-gather.3.cloned.1.call-update
  7.3 0.0 all-gather.5.cloned.1.call-start
  7.3 0.7 compare_select_fusion
  8.0 0.7 compare_and_fusion
  8.7 0.0 copy-start
  8.7 30.6 %all-gather.3.cloned.1.call-done = bf16[1504,384]{1,0:T(8,128)(2,1)} async-done(((bf16[376,384]{1,0:T(8,128)(2,1)}), bf16[1504,384]{1,0:T(8,128)(2,1)}) %all-gather.3.cloned.1.call-update) | async-done | bytes 1155088 | tf_op jit(solution)/shard_map/all_gather | solution.py:26
  39.3 3.4 %gather_fusion = bf16[376,384]{1,0:T(8,128)(2,1)S(1)} fusion(bf16[1504,384]{1,0:T(8,128)(2,1)} %all-gather.3.cloned.1.call-done, s32[1024]{0:T(1024)S(1)} %pad_clamp_fusion), kind=kCustom, calls=%fused_computation | custom fusion | bytes 579040 | tf_op jit(solution)/shard_map/jit(_take)/gather | solution.py:27
  42.7 0.1 broadcast_select_fusion
  42.9 0.0 copy-done.2
  42.9 0.9 pad_maximum_fusion
  43.7 0.0 all-gather.5.cloned.1.call-update
  43.8 0.0 copy-done
  43.8 0.0 copy-start.4
  43.8 0.0 copy-start.3
  43.8 2.6 %copy.7 = bf16[3072,384]{0,1:T(8,128)(2,1)} copy(bf16[3072,384]{1,0:T(8,128)(2,1)S(1)} %copy-done) | data formatting | bytes 4718592 | tf_op args[1]
  46.4 0.0 copy-start.1
  46.4 0.0 copy-done.4
  46.4 0.1 dynamic_slice.3
  46.5 0.0 copy-done.3
  46.5 0.3 fusion.5
  46.8 47.7 %all-gather.5.cloned.1.call-done = bf16[752,3072]{1,0:T(8,128)(2,1)} async-done(((bf16[752,384]{1,0:T(8,128)(2,1)}), bf16[752,3072]{1,0:T(8,128)(2,1)}) %all-gather.5.cloned.1.call-update) | async-done | bytes 4620304 | tf_op jit(solution)/shard_map/all_gather | solution.py:30
  94.5 0.4 mul.15
  94.9 0.0 copy-done.1
  94.9 4.9 %fusion = f32[752,384]{1,0:T(8,128)S(1)} fusion(bf16[752,3072]{1,0:T(8,128)(2,1)} %all-gather.5.cloned.1.call-done, bf16[3072,384]{0,1:T(8,128)(2,1)S(1)} %copy-done.1, bf16[48,8,24,128]{3,2,1,0:T(8,128)(2,1)S(1)} %bitcast.8), kind=kOutput, calls=%fused_computation.2 | convolution fusion | flops 1775370240 | bytes 10493952 | tf_op jit(solution)/shard_map/dot_general | solution.py:29
  99.8 0.9 slice_subtract_fusion
  (1 shorter events, 0.0 us)
Async XLA Ops:
  6.5 36.3 %copy-start.2 = (bf16[376,384]{1,0:T(8,128)(2,1)S(1)}, bf16[376,384]{1,0:T(8,128)(2,1)}, u32[]{:S(2)}) copy-start(bf16[376,384]{1,0:T(8,128)(2,1)} %param.5) | copy-start | bytes 866308
  6.5 32.8 %all-gather.3.cloned.1.call-start = ((), (), s32[]{:S(2)}) async-start(), calls=%async_computation | async-start | bytes 1443840 | tf_op jit(solution)/shard_map/all_gather | solution.py:26
  7.3 87.3 %all-gather.5.cloned.1.call-start = ((), (), s32[]{:S(2)}) async-start(), calls=%async_computation.1 | async-start | bytes 5197824 | tf_op jit(solution)/shard_map/all_gather | solution.py:30
  8.7 35.1 %copy-start = (bf16[3072,384]{1,0:T(8,128)(2,1)S(1)}, bf16[3072,384]{1,0:T(8,128)(2,1)}, u32[]{:S(2)}) copy-start(bf16[3072,384]{1,0:T(8,128)(2,1)} %param.6) | copy-start | bytes 7077892
  43.8 2.7 %copy-start.4 = (s32[24]{0:T(128)S(1)}, s32[24]{0:T(128)}, u32[]{:S(2)}) copy-start(s32[24]{0:T(128)} %param.7) | copy-start | bytes 292
  43.8 2.7 %copy-start.3 = (s32[6,6]{1,0:T(8,128)S(1)}, s32[6,6]{1,0:T(8,128)}, u32[]{:S(2)}) copy-start(s32[6,6]{1,0:T(8,128)} %param.8) | copy-start | bytes 436
  46.4 48.5 %copy-start.1 = (bf16[3072,384]{0,1:T(8,128)(2,1)S(1)}, bf16[3072,384]{0,1:T(8,128)(2,1)}, u32[]{:S(2)}) copy-start(bf16[3072,384]{0,1:T(8,128)(2,1)} %copy.7) | copy-start | bytes 7077892
Sparse Core Ops, SparseCore 0:
  9.2 30.0 all-gather.2
  43.9 50.6 all-gather.4
where the time goes:
time: 108 us
  waiting for transfers between devices  79.1 us (73%)
  between operations  13.5 us (12%)
  local copies, waits for them, and re-layouts  6.49 us (6%)
  matrix products  5.19 us (5%)
  other arithmetic  3.24 us (3%)
    all_gather x1, waiting for transfers between devices, body(): lax.all_gather(stacked, 'vir', axis=1, tiled=True)  47.7 us
    all_gather x1, waiting for transfers between devices, body(): gathered = lax.all_gather(amplitudes, 'occ', axis=0, tiled=True)  30.6 us
    dot_general x1, matrix products, body(): jnp.dot(lax.all_gather(stacked, 'vir', axis=1, tiled=True), masked, prefe...  4.88 us
    gather x1, local copies, waits for them, and re-layouts, body(): partner_rows = jnp.take(gathered, partner, axis=0)  3.4 us
    unnamed x11, local copies, waits for them, and re-layouts  2.65 us
  transfers between devices with their start and end apart: 2, of which 2 were waited for; matrix products, arithmetic and copies ran while one was open for 4% of the time, Pallas kernels for 0%

commit v1 on v0

--- a/solution.py
+++ b/solution.py
@@ -4,6 +4,16 @@
 from jax.sharding import PartitionSpec as P
 
 TILE = 128
+
+
+def collect(x, axis, dim):
+    ways, here, step = (lax.axis_size(axis), lax.axis_index(axis), x.shape[dim])
+    dims = [n * ways if d == dim else n for d, n in enumerate(x.shape)]
+    full = lax.dynamic_update_slice_in_dim(jnp.zeros(dims, x.dtype), x, here * step, axis=dim)
+    for far in range(1, ways):
+        x = lax.ppermute(x, axis, [(d, (d + 1) % ways) for d in range(ways)])
+        full = lax.dynamic_update_slice_in_dim(full, x, (here - far) % ways * step, axis=dim)
+    return full
 
 
 def body(amplitudes, integrals, tile_block, pair_mask, partner):
@@ -26,11 +36,7 @@
     gathered = lax.all_gather(amplitudes, "occ", axis=0, tiled=True)
     partner_rows = jnp.take(gathered, partner, axis=0)
     stacked = jnp.concatenate((amplitudes, partner_rows), axis=0)
-    pair_sums = jnp.dot(
-        lax.all_gather(stacked, "vir", axis=1, tiled=True),
-        masked,
-        preferred_element_type=jnp.float32,
-    )
+    pair_sums = jnp.dot(collect(stacked, "vir", 1), masked, preferred_element_type=jnp.float32)
     residual = pair_sums[:own_count] - pair_sums[own_count:]
     return residual
 

time: 108 us -> 140 us (1.30)
  waiting for transfers between devices: 79.1 us -> 95.9 us
  local copies, waits for them, and re-layouts: 6.49 us -> 21.6 us
    ppermute x0 -> x7, waiting for transfers between devices: none -> 64.5 us  [collect(): x = lax.ppermute(x, axis, [(d, (d + 1) % ways) for d in range(ways)])]
    all_gather x1 -> x0, waiting for transfers between devices: 47.7 us -> none  [body(): lax.all_gather(stacked, 'vir', axis=1, tiled=True)]
    dynamic_update_slice x0 -> x7, local copies, waits for them, and re-layouts: none -> 10.8 us  [collect(): lax.dynamic_update_slice_in_dim(full, x, (here - far) % ways * step, axis...]
    broadcast_in_dim x0 -> x1, local copies, waits for them, and re-layouts: none -> 2.68 us  [collect(): jnp.zeros(dims, x.dtype)]
    unnamed x11 -> x15, local copies, waits for them, and re-layouts: 2.65 us -> 4.33 us
  transfers between devices with their start and end apart: 2 -> 8, of which waited for: 2 -> 8; matrix products, arithmetic and copies ran while one was open for 4% -> 10% of each run, Pallas kernels for 0% -> 0%
where the time goes in v1:
time: 140 us
  waiting for transfers between devices  95.9 us (68%)
  local copies, waits for them, and re-layouts  21.6 us (15%)
  between operations  13.5 us (10%)
  matrix products  5.26 us (4%)
  other arithmetic  3.39 us (2%)
    ppermute x7, waiting for transfers between devices, collect(): x = lax.ppermute(x, axis, [(d, (d + 1) % ways) for d in range(ways)])  64.5 us
    all_gather x1, waiting for transfers between devices, body(): gathered = lax.all_gather(amplitudes, 'occ', axis=0, tiled=True)  30.7 us
    dynamic_update_slice x7, local copies, waits for them, and re-layouts, collect(): lax.dynamic_update_slice_in_dim(full, x, (here - far) % ways * step, axis...  10.8 us
    dot_general x1, matrix products, body(): jnp.dot(collect(stacked, 'vir', 1), masked, preferred_element_type=jnp.fl...  4.96 us
    unnamed x15, local copies, waits for them, and re-layouts  4.33 us
    gather x1, local copies, waits for them, and re-layouts, body(): partner_rows = jnp.take(gathered, partner, axis=0)  3.4 us
  transfers between devices with their start and end apart: 8, of which 8 were waited for; matrix products, arithmetic and copies ran while one was open for 10% of the time, Pallas kernels for 0%

profile of v1, /device:TPU:0, one launch (start us, length us, event | category | flops | bytes accessed | tf_op | source)
XLA Modules:
  0.0 139.7 jit_solution(12087572415335985815)
XLA Ops:
  6.5 0.0 copy-start.2
  6.5 0.0 all-gather.2.cloned.1.call-start
  6.5 0.7 all-gather.2.cloned.1.call-update
  7.3 0.7 compare_select_fusion
  8.0 0.7 compare_and_fusion
  8.6 0.0 copy-start
  8.6 30.7 %all-gather.2.cloned.1.call-done = bf16[1504,384]{1,0:T(8,128)(2,1)} async-done(((bf16[376,384]{1,0:T(8,128)(2,1)}), bf16[1504,384]{1,0:T(8,128)(2,1)}) %all-gather.2.cloned.1.call-update) | async-done | bytes 1155088 | tf_op jit(solution)/shard_map/all_gather | solution.py:36
  39.3 3.4 %gather_fusion = bf16[376,384]{1,0:T(8,128)(2,1)S(1)} fusion(bf16[1504,384]{1,0:T(8,128)(2,1)} %all-gather.2.cloned.1.call-done, s32[1024]{0:T(1024)S(1)} %pad_clamp_fusion), kind=kCustom, calls=%fused_computation | custom fusion | bytes 579040 | tf_op jit(solution)/shard_map/jit(_take)/gather | solution.py:37
  42.7 0.1 broadcast_select_fusion
  42.9 0.0 copy-start.6
  42.9 0.0 copy-start.5
  42.9 2.7 %broadcast_in_dim.20 = bf16[752,3072]{1,0:T(8,128)(2,1)} broadcast(bf16[]{:T(256)} %constant.68.clone.1), dimensions={} | broadcast | bytes 4620290 | tf_op jit(solution)/shard_map/broadcast_in_dim | solution.py:12
  45.6 0.0 copy-done.2
  45.6 1.0 pad_maximum_fusion
  46.6 0.0 collective-permute-start
  46.6 11.0 %collective-permute-done = bf16[752,384]{1,0:T(8,128)(2,1)S(1)} collective-permute-done((bf16[752,384]{1,0:T(8,128)(2,1)S(1)}, bf16[752,384]{1,0:T(8,128)(2,1)S(1)}, u32[]{:S(2)}, u32[]{:S(2)}) %collective-permute-start) | collective-permute-done | bytes 577568 | tf_op jit(solution)/shard_map/ppermute | solution.py:14
  57.6 0.0 collective-permute-start.1
  57.6 11.0 %collective-permute-done.1 = bf16[752,384]{1,0:T(8,128)(2,1)S(1)} collective-permute-done((bf16[752,384]{1,0:T(8,128)(2,1)S(1)}, bf16[752,384]{1,0:T(8,128)(2,1)S(1)}, u32[]{:S(2)}, u32[]{:S(2)}) %collective-permute-start.1) | collective-permute-done | bytes 577568 | tf_op jit(solution)/shard_map/ppermute | solution.py:14
  68.5 0.0 collective-permute-start.2
  68.5 11.0 %collective-permute-done.2 = bf16[752,384]{1,0:T(8,128)(2,1)S(1)} collective-permute-done((bf16[752,384]{1,0:T(8,128)(2,1)S(1)}, bf16[752,384]{1,0:T(8,128)(2,1)S(1)}, u32[]{:S(2)}, u32[]{:S(2)}) %collective-permute-start.2) | collective-permute-done | bytes 577568 | tf_op jit(solution)/shard_map/ppermute | solution.py:14
  79.5 0.0 copy-start.3
  79.5 0.8 copy-done.3
  80.3 0.0 collective-permute-start.3
  80.3 11.0 %collective-permute-done.3 = bf16[752,384]{1,0:T(8,128)(2,1)S(1)} collective-permute-done((bf16[752,384]{1,0:T(8,128)(2,1)S(1)}, bf16[752,384]{1,0:T(8,128)(2,1)S(1)}, u32[]{:S(2)}, u32[]{:S(2)}) %collective-permute-start.3) | collective-permute-done | bytes 577568 | tf_op jit(solution)/shard_map/ppermute | solution.py:14
  91.3 0.0 copy-start.4
  91.3 0.8 copy-done.4
  92.1 0.0 collective-permute-start.4
  92.1 11.1 %collective-permute-done.4 = bf16[752,384]{1,0:T(8,128)(2,1)} collective-permute-done((bf16[752,384]{1,0:T(8,128)(2,1)S(1)}, bf16[752,384]{1,0:T(8,128)(2,1)}, u32[]{:S(2)}, u32[]{:S(2)}) %collective-permute-start.4) | collective-permute-done | bytes 577568 | tf_op jit(solution)/shard_map/ppermute | solution.py:14
  103.2 0.0 collective-permute-start.5
  103.2 0.0 copy-done
  103.2 2.6 %copy.7 = bf16[3072,384]{0,1:T(8,128)(2,1)} copy(bf16[3072,384]{1,0:T(8,128)(2,1)S(1)} %copy-done) | data formatting | bytes 4718592 | tf_op args[1]
  105.9 0.0 copy-done.6
  105.9 0.1 dynamic_slice.3
  106.0 0.0 copy-done.5
  106.0 0.3 fusion.5
  106.3 0.9 constant_dynamic-update-slice_fusion.6
  107.2 0.0 copy-start.1
  107.2 7.3 %collective-permute-done.5 = bf16[752,384]{1,0:T(8,128)(2,1)} collective-permute-done((bf16[752,384]{1,0:T(8,128)(2,1)}, bf16[752,384]{1,0:T(8,128)(2,1)}, u32[]{:S(2)}, u32[]{:S(2)}) %collective-permute-start.5) | collective-permute-done | bytes 577568 | tf_op jit(solution)/shard_map/ppermute | solution.py:14
  114.5 0.0 collective-permute-start.6
  114.5 0.9 constant_dynamic-update-slice_fusion.5
  115.5 2.0 %constant_dynamic-update-slice_fusion.4 = bf16[752,3072]{1,0:T(8,128)(2,1)} fusion(bf16[752,3072]{1,0:T(8,128)(2,1)} %constant_dynamic-update-slice_fusion.5, bf16[752,384]{1,0:T(8,128)(2,1)} %copy-done.3, s32[]{:T(128)S(6)} %select_n.75), kind=kLoop, calls=%fused_computation.20 | loop fusion | bytes 1155076 | tf_op jit(solution)/shard_map/dynamic_update_slice | solution.py:15
  117.5 2.0 %constant_dynamic-update-slice_fusion.3 = bf16[752,3072]{1,0:T(8,128)(2,1)} fusion(bf16[752,3072]{1,0:T(8,128)(2,1)} %constant_dynamic-update-slice_fusion.4, bf16[752,384]{1,0:T(8,128)(2,1)} %copy-done.4, s32[]{:T(128)S(6)} %select_n.77), kind=kLoop, calls=%fused_computation.19 | loop fusion | bytes 1155076 | tf_op jit(solution)/shard_map/dynamic_update_slice | solution.py:15
  119.4 2.0 %constant_dynamic-update-slice_fusion.2 = bf16[752,3072]{1,0:T(8,128)(2,1)} fusion(bf16[752,3072]{1,0:T(8,128)(2,1)} %constant_dynamic-update-slice_fusion.3, bf16[752,384]{1,0:T(8,128)(2,1)} %collective-permute-done.4, s32[]{:T(128)S(6)} %select_n.79), kind=kLoop, calls=%fused_computation.18 | loop fusion | bytes 1155076 | tf_op jit(solution)/shard_map/dynamic_update_slice | solution.py:15
  121.5 2.0 %constant_dynamic-update-slice_fusion.1 = bf16[752,3072]{1,0:T(8,128)(2,1)} fusion(bf16[752,3072]{1,0:T(8,128)(2,1)} %constant_dynamic-update-slice_fusion.2, bf16[752,384]{1,0:T(8,128)(2,1)} %collective-permute-done.5, s32[]{:T(128)S(6)} %select_n.81), kind=kLoop, calls=%fused_computation.17 | loop fusion | bytes 1155076 | tf_op jit(solution)/shard_map/dynamic_update_slice | solution.py:15
  123.5 2.2 %collective-permute-done.6 = bf16[752,384]{1,0:T(8,128)(2,1)S(1)} collective-permute-done((bf16[752,384]{1,0:T(8,128)(2,1)}, bf16[752,384]{1,0:T(8,128)(2,1)S(1)}, u32[]{:S(2)}, u32[]{:S(2)}) %collective-permute-start.6) | collective-permute-done | bytes 577568 | tf_op jit(solution)/shard_map/ppermute | solution.py:14
  125.7 0.9 constant_dynamic-update-slice_fusion
  126.6 0.4 mul.47
  127.0 0.0 copy-done.1
  127.0 5.0 %fusion = f32[752,384]{1,0:T(8,128)S(1)} fusion(bf16[752,3072]{1,0:T(8,128)(2,1)} %constant_dynamic-update-slice_fusion, bf16[3072,384]{0,1:T(8,128)(2,1)S(1)} %copy-done.1, bf16[48,8,24,128]{3,2,1,0:T(8,128)(2,1)S(1)} %bitcast.8), kind=kOutput, calls=%fused_computation.2 | convolution fusion | flops 1775370240 | bytes 10493952 | tf_op jit(solution)/shard_map/dot_general | solution.py:39
  131.9 0.9 slice_subtract_fusion
  (1 shorter events, 0.0 us)
Async XLA Ops:
  6.5 39.0 %copy-start.2 = (bf16[376,384]{1,0:T(8,128)(2,1)S(1)}, bf16[376,384]{1,0:T(8,128)(2,1)}, u32[]{:S(2)}) copy-start(bf16[376,384]{1,0:T(8,128)(2,1)} %param.5) | copy-start | bytes 866308
  6.5 32.8 %all-gather.2.cloned.1.call-start = ((), (), s32[]{:S(2)}) async-start(), calls=%async_computation | async-start | bytes 1443840 | tf_op jit(solution)/shard_map/all_gather | solution.py:36
  8.6 94.6 %copy-start = (bf16[3072,384]{1,0:T(8,128)(2,1)S(1)}, bf16[3072,384]{1,0:T(8,128)(2,1)}, u32[]{:S(2)}) copy-start(bf16[3072,384]{1,0:T(8,128)(2,1)} %param.6) | copy-start | bytes 7077892
  42.9 63.0 %copy-start.6 = (s32[24]{0:T(128)S(1)}, s32[24]{0:T(128)}, u32[]{:S(2)}) copy-start(s32[24]{0:T(128)} %param.7) | copy-start | bytes 292
  42.9 63.1 %copy-start.5 = (s32[6,6]{1,0:T(8,128)S(1)}, s32[6,6]{1,0:T(8,128)}, u32[]{:S(2)}) copy-start(s32[6,6]{1,0:T(8,128)} %param.8) | copy-start | bytes 436
  46.6 11.0 %collective-permute-start = (bf16[752,384]{1,0:T(8,128)(2,1)S(1)}, bf16[752,384]{1,0:T(8,128)(2,1)S(1)}, u32[]{:S(2)}, u32[]{:S(2)}) collective-permute-start(bf16[752,384]{1,0:T(8,128)(2,1)S(1)} %get-tuple-element.5), channel_id=1, source_target_pairs={{0,1},{1,2},{2,3},{3,4},{4,5},{5,6},{6,7},{7,0},{8,9},{9,10},{10,1... | collective-permute-start | bytes 1732616 | tf_op jit(solution)/shard_map/ppermute | solution.py:14
  57.6 11.0 %collective-permute-start.1 = (bf16[752,384]{1,0:T(8,128)(2,1)S(1)}, bf16[752,384]{1,0:T(8,128)(2,1)S(1)}, u32[]{:S(2)}, u32[]{:S(2)}) collective-permute-start(bf16[752,384]{1,0:T(8,128)(2,1)S(1)} %collective-permute-done), channel_id=1, source_target_pairs={{0,1},{1,2},{2,3},{3,4},{4,5},{5,6},{6,7},{7,0},{8,9},{9,10},{10,1... | collective-permute-start | bytes 1732616 | tf_op jit(solution)/shard_map/ppermute | solution.py:14
  68.5 11.0 %collective-permute-start.2 = (bf16[752,384]{1,0:T(8,128)(2,1)S(1)}, bf16[752,384]{1,0:T(8,128)(2,1)S(1)}, u32[]{:S(2)}, u32[]{:S(2)}) collective-permute-start(bf16[752,384]{1,0:T(8,128)(2,1)S(1)} %collective-permute-done.1), channel_id=1, source_target_pairs={{0,1},{1,2},{2,3},{3,4},{4,5},{5,6},{6,7},{7,0},{8,9},{9,10},{10,1... | collective-permute-start | bytes 1732616 | tf_op jit(solution)/shard_map/ppermute | solution.py:14
  79.5 0.8 copy-start.3
  80.3 11.0 %collective-permute-start.3 = (bf16[752,384]{1,0:T(8,128)(2,1)S(1)}, bf16[752,384]{1,0:T(8,128)(2,1)S(1)}, u32[]{:S(2)}, u32[]{:S(2)}) collective-permute-start(bf16[752,384]{1,0:T(8,128)(2,1)S(1)} %collective-permute-done.2), channel_id=1, source_target_pairs={{0,1},{1,2},{2,3},{3,4},{4,5},{5,6},{6,7},{7,0},{8,9},{9,10},{10,1... | collective-permute-start | bytes 1732616 | tf_op jit(solution)/shard_map/ppermute | solution.py:14
  91.3 0.9 copy-start.4
  92.1 11.1 %collective-permute-start.4 = (bf16[752,384]{1,0:T(8,128)(2,1)S(1)}, bf16[752,384]{1,0:T(8,128)(2,1)}, u32[]{:S(2)}, u32[]{:S(2)}) collective-permute-start(bf16[752,384]{1,0:T(8,128)(2,1)S(1)} %collective-permute-done.3), channel_id=1, source_target_pairs={{0,1},{1,2},{2,3},{3,4},{4,5},{5,6},{6,7},{7,0},{8,9},{9,10},{10,1... | collective-permute-start | bytes 1732616 | tf_op jit(solution)/shard_map/ppermute | solution.py:14
  103.2 11.3 %collective-permute-start.5 = (bf16[752,384]{1,0:T(8,128)(2,1)}, bf16[752,384]{1,0:T(8,128)(2,1)}, u32[]{:S(2)}, u32[]{:S(2)}) collective-permute-start(bf16[752,384]{1,0:T(8,128)(2,1)} %collective-permute-done.4), channel_id=1, source_target_pairs={{0,1},{1,2},{2,3},{3,4},{4,5},{5,6},{6,7},{7,0},{8,9},{9,10},{10,1... | collective-permute-start | bytes 1732616 | tf_op jit(solution)/shard_map/ppermute | solution.py:14
  107.2 19.8 %copy-start.1 = (bf16[3072,384]{0,1:T(8,128)(2,1)S(1)}, bf16[3072,384]{0,1:T(8,128)(2,1)}, u32[]{:S(2)}) copy-start(bf16[3072,384]{0,1:T(8,128)(2,1)} %copy.7) | copy-start | bytes 7077892
  114.5 11.2 %collective-permute-start.6 = (bf16[752,384]{1,0:T(8,128)(2,1)}, bf16[752,384]{1,0:T(8,128)(2,1)S(1)}, u32[]{:S(2)}, u32[]{:S(2)}) collective-permute-start(bf16[752,384]{1,0:T(8,128)(2,1)} %collective-permute-done.5), channel_id=1, source_target_pairs={{0,1},{1,2},{2,3},{3,4},{4,5},{5,6},{6,7},{7,0},{8,9},{9,10},{10,1... | collective-permute-start | bytes 1732616 | tf_op jit(solution)/shard_map/ppermute | solution.py:14
Sparse Core Ops, SparseCore 0:
  9.2 30.0 all-gather.1
